TPU v7x, 256 devices: a whole 4x4x8 slice. The times are simulated.
256 devices in a mesh: cfg: 2 (over y_hi), seq: 128 (over y_lo, x, z, core).
Axes of the slice: x: 4, y: 4 (y_hi: 2, y_lo: 2; y = y_hi * 2 + y_lo), z: 8, core: 2. Of those that a mesh axis runs over, the one named last changes fastest.
Arguments:
- hidden: bfloat16 [2, 6144, 3072], P('cfg', 'seq'), may hold values from -3 to 3
- queries: bfloat16 [2, 6144, 2048], P('cfg', 'seq'), may hold values from -5 to 5
- key_proj: bfloat16 [2, 6144, 2048], P('cfg', 'seq'), may hold values from -5 to 5
- value_proj: bfloat16 [2, 6144, 2048], P('cfg', 'seq'), may hold values from -12 to 12
- norm_gain: float32 [2, 64], replicated, may hold values from 0.1 to 1.9
- norm_bias: float32 [2, 64], replicated, may hold values from -2 to 2
- positions: int32 [3, 6144], P(None, 'seq'), may hold values from 0 to 47
- text_len: int32 [2], P('cfg'), may hold values from 1 to 226
- time_embed: bfloat16 [512], replicated, may hold values from -6 to 6
- gate_table: bfloat16 [512, 3072], P(None, 'seq'), may hold values from -0.25 to 0.25
- mod_table: bfloat16 [512, 6144], P(None, 'seq'), may hold values from -0.25 to 0.25
- out_weight: bfloat16 [2048, 3072], P(None, ('cfg', 'seq')), may hold values from -0.125 to 0.125
- proj_weight: bfloat16 [3072, 64], replicated, may hold values from -0.109375 to 0.109375
- proj_bias: float32 [64], replicated, may hold values from -3 to 3
- latent: float32 [6144, 64], P('seq'), may hold values from -6 to 6
- solver_coef: float32 [2, 50], replicated, may hold values from 0.3 to 1.2
- step_index: int32 [1], replicated, may hold values from 0 to 49
Outputs:
- latent_next: float32 [6144, 64], P('seq', 'cfg')
All inputs are finite; a program needn't handle non-finite values.
Results may differ from a plain program's by a relative error of at most 0.0072.
Values may be sent and summed in bfloat16 or wider, within the bound.
No kernel may reach another device: no remote copies, remote signals or barrier semaphores. Data moves between devices by JAX's collectives and lax.ppermute only.
A program may use at most 128 MiB of HBM per device.

v0:
```python
import math
import jax
import jax.numpy as jnp
import numpy as np
from jax import lax
from jax.sharding import PartitionSpec as P

TEXT_SLOTS = 256
GUIDANCE = 6.0


def swapped(value, axis, bit):
    return lax.ppermute(value, axis, [(i, i ^ 1 << bit) for i in range(lax.axis_size(axis))])


def layer_norm(values, epsilon):
    centre = jnp.mean(values, axis=-1, keepdims=True)
    centred = values - centre
    variance = jnp.mean(centred * centred, axis=-1, keepdims=True)
    return centred * lax.rsqrt(variance + epsilon)


def rotary_angles(positions):
    pos_float = positions.astype(jnp.float32)
    time_freq = jnp.asarray(10000.0 ** (-2.0 * np.arange(8) / 16.0), jnp.float32)
    space_freq = jnp.asarray(10000.0 ** (-2.0 * np.arange(12) / 24.0), jnp.float32)
    return jnp.concatenate(
        [
            pos_float[0][:, None] * time_freq[None, :],
            pos_float[1][:, None] * space_freq[None, :],
            pos_float[2][:, None] * space_freq[None, :],
        ],
        axis=1,
    )


def norm_rotate(values, gain_row, offset, angles, is_video):
    row_count = values.shape[0]
    head_count = values.shape[1] // 64
    normed = (
        layer_norm(values.astype(jnp.float32).reshape(row_count, head_count, 64), 1e-06) * gain_row
        + offset
    )
    paired = normed.reshape(row_count, head_count, 32, 2)
    first_half = paired[..., 0]
    second = paired[..., 1]
    cosine = jnp.cos(angles)[:, None, :]
    sine_part = jnp.sin(angles)[:, None, :]
    rotated = jnp.stack(
        [first_half * cosine - second * sine_part, first_half * sine_part + second * cosine],
        axis=-1,
    ).reshape(row_count, head_count, 64)
    return jnp.where(is_video[:, None, None], rotated, normed).astype(jnp.bfloat16)


def on_device(
    hidden,
    queries,
    key_proj,
    value_proj,
    norm_gain,
    norm_bias,
    positions,
    text_len,
    time_embed,
    gate_table,
    mod_table,
    out_weight,
    proj_weight,
    proj_bias,
    latent,
    solver_coef,
    step_index,
):
    seq_count = lax.axis_size("seq")
    seq_place = lax.axis_index("seq")
    local_rows = queries.shape[1]
    head_count = queries.shape[2] // 64
    head_group = max(head_count // seq_count, 1)
    row_split = max(seq_count // head_count, 1)
    part_rows = local_rows // row_split
    head_sets = head_count // head_group
    row_index = seq_place * local_rows + jnp.arange(local_rows)
    is_video = row_index >= TEXT_SLOTS
    angles = rotary_angles(positions)
    rot_query = norm_rotate(queries[0], norm_gain[0], norm_bias[0], angles, is_video)
    rot_key = norm_rotate(key_proj[0], norm_gain[1], norm_bias[1], angles, is_video)
    query_send = rot_query.reshape(row_split, part_rows, head_sets, head_group, 64)
    query_send = query_send.transpose(2, 0, 1, 3, 4).reshape(seq_count, part_rows * head_group * 64)

    def spread(values):
        grouped = values.transpose(1, 0, 2)
        widened = jnp.broadcast_to(
            grouped[:, None], (head_sets, row_split, local_rows, head_group * 64)
        )
        return widened.reshape(seq_count, local_rows * head_group * 64)

    key_send = spread(rot_key)
    value_send = spread(value_proj[0].reshape(local_rows, head_count, 64))
    query_recv, key_recv, value_recv = (
        lax.all_to_all(query_send, "seq", split_axis=0, concat_axis=0, tiled=True),
        lax.all_to_all(key_send, "seq", split_axis=0, concat_axis=0, tiled=True),
        lax.all_to_all(value_send, "seq", split_axis=0, concat_axis=0, tiled=True),
    )
    total_keys = seq_count * local_rows
    query_count = seq_count * part_rows
    query_all = query_recv.reshape(query_count, head_group, 64)
    key_index = jnp.arange(total_keys)
    key_valid = (key_index >= TEXT_SLOTS) | (key_index < text_len[0])
    block_keys = math.gcd(512, total_keys)
    block_count = total_keys // block_keys

    def key_step(state_pair, operands):
        numerator, denominator = state_pair
        key_block, value_block, valid_block = operands
        scores = (
            jnp.einsum("qgd,kgd->gqk", query_all, key_block, preferred_element_type=jnp.float32)
            * 0.125
        )
        weights = jnp.where(valid_block[None, None, :], jnp.exp(scores), 0.0)
        denominator = denominator + jnp.sum(weights, axis=2)
        numerator = numerator + jnp.einsum(
            "gqk,kgd->gqd",
            weights.astype(jnp.bfloat16),
            value_block,
            preferred_element_type=jnp.float32,
        )
        return ((numerator, denominator), None)

    start_state = (
        jnp.zeros((head_group, query_count, 64), jnp.float32),
        jnp.zeros((head_group, query_count), jnp.float32),
    )
    scanned = (
        key_recv.reshape(block_count, block_keys, head_group, 64),
        value_recv.reshape(block_count, block_keys, head_group, 64),
        key_valid.reshape(block_count, block_keys),
    )
    final_state, unused_out = lax.scan(key_step, start_state, scanned)
    attended = (final_state[0] / final_state[1][..., None]).astype(jnp.bfloat16)
    back_send = attended.reshape(head_group, seq_count, part_rows, 64).transpose(1, 2, 0, 3)
    back_send = back_send.reshape(seq_count, part_rows * head_group * 64)
    back_recv = lax.all_to_all(back_send, "seq", split_axis=0, concat_axis=0, tiled=True)
    attended_rows = back_recv.reshape(head_sets, row_split, part_rows, head_group, 64)
    attended_rows = attended_rows.transpose(1, 2, 0, 3, 4).reshape(local_rows, head_count * 64)
    embed_act = jax.nn.silu(time_embed.astype(jnp.float32)).astype(jnp.bfloat16)[None, :]
    gate_full, mod_full = (
        lax.all_gather(gate_table, "seq", axis=1, tiled=True),
        lax.all_gather(mod_table, "seq", axis=1, tiled=True),
    )
    gate_vec = jnp.dot(embed_act, gate_full, preferred_element_type=jnp.float32)[0]
    modulation = jnp.dot(embed_act, mod_full, preferred_element_type=jnp.float32)[0]
    projected = jnp.dot(
        attended_rows,
        lax.all_gather(out_weight, ("cfg", "seq"), axis=1, tiled=True),
        preferred_element_type=jnp.float32,
    )
    model_width = hidden.shape[2]
    residual = hidden[0].astype(jnp.float32) + gate_vec[None, :] * projected
    normed = (
        layer_norm(residual, 1e-05) * (1.0 + modulation[model_width:]) + modulation[:model_width]
    )
    normed = normed.astype(jnp.bfloat16)
    prediction = jnp.dot(normed, proj_weight, preferred_element_type=jnp.float32) + proj_bias
    cfg_place = lax.axis_index("cfg")
    own_width = prediction.shape[1] // 2
    own_pred = lax.dynamic_slice_in_dim(prediction, cfg_place * own_width, own_width, 1)
    sent_pred = lax.dynamic_slice_in_dim(prediction, (1 - cfg_place) * own_width, own_width, 1)
    partner = swapped(sent_pred, "cfg", 0)
    is_cond = cfg_place == 0
    cond_pred = jnp.where(is_cond, own_pred, partner)
    uncond_pred = jnp.where(is_cond, partner, own_pred)
    guided = uncond_pred + GUIDANCE * (cond_pred - uncond_pred)
    own_latent = lax.dynamic_slice_in_dim(latent, cfg_place * own_width, own_width, 1)
    step_coefs = lax.dynamic_index_in_dim(solver_coef, step_index[0], axis=1, keepdims=False)
    updated = step_coefs[0] * own_latent + step_coefs[1] * guided
    return jnp.where(is_video[:, None], updated, 0.0)


def solution(mesh):
    placed = (
        P("cfg", "seq", None),
        P("cfg", "seq", None),
        P("cfg", "seq", None),
        P("cfg", "seq", None),
        P(),
        P(),
        P(None, "seq"),
        P("cfg"),
        P(),
        P(None, "seq"),
        P(None, "seq"),
        P(None, ("cfg", "seq")),
        P(),
        P(),
        P("seq", None),
        P(),
        P(),
    )
    return jax.shard_map(
        on_device, mesh=mesh, in_specs=placed, out_specs=P("seq", "cfg"), check_vma=False
    )
```

profile of v0, /device:TPU:1, one launch (start us, length us, event | category | flops | bytes accessed | tf_op | source)
XLA Modules:
  0.0 621.5 jit_solution(9374460455169536504)
XLA Ops:
  8.8 1.2 copy.94
  10.1 0.9 copy.96
  15.2 0.8 multiply_add_fusion
  16.0 0.8 multiply_add_fusion.1
  16.8 3.5 multiply_subtract_fusion
  20.3 1.4 pad_maximum_fusion.1
  21.7 2.1 copy.95
  23.8 2.2 reshape.328
  26.1 1.6 copy.98
  27.7 1.3 rsqrt.30
  29.0 1.3 div.39
  30.4 2.8 fusion.14
  33.2 2.0 copy.100
  36.1 1.8 reduce.27
  38.7 15.3 %all-to-all-start.1 = ((bf16[128,2,384]{2,1,0:T(2,128)(2,1)}), bf16[128,2,384]{2,1,0:T(2,128)(2,1)}, u32[]{:S(2)}, u32[]{:S(2)}) async-start(bf16[128,2,384]{2,1,0:T(2,128)(2,1)} %reshape.368), calls=%async_computation.1 | async-start | bytes 393216 | tf_op jit(solution)/shard_map/all_to_all | solution.py:101
  54.0 1.4 pad_maximum_fusion
  56.1 0.8 fusion.13
  57.7 0.9 all_to_all.32
  58.5 5.3 reduce.26
  63.9 1.5 reshape.366
  65.4 0.8 all-to-all-done.1
  66.2 12.1 %all-to-all-start = ((bf16[128,2,1536]{2,1,0:T(2,128)(2,1)}), bf16[128,2,1536]{2,1,0:T(2,128)(2,1)}, u32[]{:S(2)}, u32[]{:S(2)}) async-start(bf16[128,2,1536]{2,1,0:T(2,128)(2,1)} %reshape.366), calls=%async_computation | async-start | bytes 1572864 | tf_op jit(solution)/shard_map/all_to_all | solution.py:102
  79.0 0.9 all_to_all.34
  79.8 5.3 reduce.28
  85.2 1.5 reshape.370
  86.6 15.1 %all-to-all-done = bf16[128,2,1536]{2,1,0:T(2,128)(2,1)} async-done(((bf16[128,2,1536]{2,1,0:T(2,128)(2,1)}), bf16[128,2,1536]{2,1,0:T(2,128)(2,1)}, u32[]{:S(2)}, u32[]{:S(2)}) %all-to-all-start) | async-done | bytes 786464 | tf_op jit(solution)/shard_map/all_to_all | solution.py:102
  101.8 8.7 %all-to-all-start.2 = ((bf16[128,2,1536]{2,1,0:T(2,128)(2,1)}), bf16[128,2,1536]{2,1,0:T(2,128)(2,1)}, u32[]{:S(2)}, u32[]{:S(2)}) async-start(bf16[128,2,1536]{2,1,0:T(2,128)(2,1)} %reshape.370), calls=%async_computation.2 | async-start | bytes 1572864 | tf_op jit(solution)/shard_map/all_to_all | solution.py:103
  111.2 1.6 reshape.369
  112.7 1.2 reduce.9
  114.3 5.0 reshape.367
  119.3 4.7 reduce.6
  124.1 1.0 reshape.317
  125.1 1.4 copy.104
  126.5 7.3 %all-to-all-done.2 = bf16[128,2,1536]{2,1,0:T(2,128)(2,1)} async-done(((bf16[128,2,1536]{2,1,0:T(2,128)(2,1)}), bf16[128,2,1536]{2,1,0:T(2,128)(2,1)}, u32[]{:S(2)}, u32[]{:S(2)}) %all-to-all-start.2) | async-done | bytes 786464 | tf_op jit(solution)/shard_map/all_to_all | solution.py:103
  133.8 5.3 reshape.371
  139.1 4.7 reduce.10
  143.8 1.0 reshape.320
  145.5 25.9 %while.13 = (s32[]{:T(128)}, f32[1,1536,64]{1,2,0:T(8,128)S(1)}, f32[1,1536]{1,0:T(1,128)S(1)}, pred[12,512]{1,0:T(8,128)(4,1)S(1)}, bf16[12,512,1,64]{1,3,2,0:T...) while((s32[]{:T(128)}, f32[1,1536,64]{1,2,0:T(8,128)S(1)}, ...), condition=%wide.region_6.7_spmd.clone, body=%wide.region_4.6_spmd.clone.sunk | while | flops 204670464 | bytes 4286076 | solution.py:139
  145.6 1.6 fusion.47
  147.7 1.7 fusion.47
  149.9 1.7 fusion.47
  152.0 1.6 fusion.47
  154.2 1.6 fusion.47
  156.4 1.6 fusion.47
  158.5 1.6 fusion.47
  160.7 1.6 fusion.47
  162.9 1.6 fusion.47
  165.0 1.6 fusion.47
  167.2 1.6 fusion.47
  169.3 1.6 fusion.47
  172.0 1.8 reduce.29
  174.5 8.3 %all-to-all-start.3 = ((bf16[128,2,384]{2,1,0:T(2,128)(2,1)}), bf16[128,2,384]{2,1,0:T(2,128)(2,1)S(1)}, u32[]{:S(2)}, u32[]{:S(2)}) async-start(bf16[128,2,384]{2,1,0:T(2,128)(2,1)} %reshape.372), calls=%async_computation.3 | async-start | bytes 393216 | tf_op jit(solution)/shard_map/all_to_all | solution.py:143
  183.6 11.7 %all-to-all-done.3 = bf16[128,2,384]{2,1,0:T(2,128)(2,1)S(1)} async-done(((bf16[128,2,384]{2,1,0:T(2,128)(2,1)}), bf16[128,2,384]{2,1,0:T(2,128)(2,1)S(1)}, u32[]{:S(2)}, u32[]{:S(2)}) %all-to-all-start.3) | async-done | bytes 196640 | tf_op jit(solution)/shard_map/all_to_all | solution.py:143
  195.4 1.2 reduce.12
  197.6 33.6 %all-gather.5.cloned.1.call-done = bf16[512,3072]{0,1:T(8,128)(2,1)} async-done(((bf16[512,24]{0,1:T(8,128)(2,1)}), bf16[512,3072]{0,1:T(8,128)(2,1)}) %all-gather.5.cloned.1.call-update) | async-done | bytes 3145744 | tf_op jit(solution)/shard_map/all_gather | solution.py:148
  231.2 2.8 fusion.30
  234.0 215.7 %all-gather.7.cloned.1.call-done = bf16[512,6144]{0,1:T(8,128)(2,1)} async-done(((bf16[512,48]{0,1:T(8,128)(2,1)}), bf16[512,6144]{0,1:T(8,128)(2,1)}) %all-gather.7.cloned.1.call-update) | async-done | bytes 6291472 | tf_op jit(solution)/shard_map/all_gather | solution.py:149
  449.7 4.5 fusion.31
  454.2 124.8 %all-gather.9.cloned.1.call-done = bf16[256,12,2048]{2,1,0:T(8,128)(2,1)} async-done(((bf16[1,12,2048]{2,1,0:T(8,128)(2,1)}), bf16[256,12,2048]{2,1,0:T(8,128)(2,1)}) %all-gather.9.cloned.1.call-update) | async-done | bytes 12582928 | tf_op jit(solution)/shard_map/all_gather | solution.py:155
  579.0 19.9 %reshape.330 = bf16[3072,2048]{1,0:T(8,128)(2,1)} reshape(bf16[256,12,2048]{2,1,0:T(8,128)(2,1)} %all-gather.9.cloned.1.call-done) | data formatting | bytes 25165824
  598.9 8.6 %fusion.29 = (f32[48]{0:T(128)S(1)}, f32[48,3072]{1,0:T(8,128)S(1)}) fusion(bf16[48,2048]{1,0:T(8,128)(2,1)S(1)} %reshape.322, bf16[3072,2048]{1,0:T(8,128)(2,1)} %reshape.330, f32[3072]{0:T(1024)S(1)} %bitcast.102, bf16[1,48,3072]{2,1,0:T(8,128)(2,1)S(1)} %copy-done.2), kind=kOutput, calls=%fused_computation.81 | convolution fusion | flops 604569536 | bytes 13676736 | tf_op jit(solution)/shard_map/dot_general | solution.py:153
  608.2 2.8 collective-permute-start
  611.6 0.9 collective-permute-done
  612.4 1.4 add_select_fusion
  (142 shorter events, 21.2 us)
Async XLA Ops:
  6.5 601.2 %copy-start = (bf16[3072,64]{0,1:T(8,128)(2,1)S(1)}, bf16[3072,64]{0,1:T(8,128)(2,1)}, u32[]{:S(2)}) copy-start(bf16[3072,64]{0,1:T(8,128)(2,1)} %param.33) | copy-start | bytes 1179652
  6.5 224.7 %all-gather.5.cloned.1.call-start = ((), (), s32[]{:S(2)}) async-start(), calls=%async_computation.4 | async-start | bytes 3170304 | tf_op jit(solution)/shard_map/all_gather | solution.py:148
  7.3 442.4 %all-gather.7.cloned.1.call-start = ((), (), s32[]{:S(2)}) async-start(), calls=%async_computation.5 | async-start | bytes 6340608 | tf_op jit(solution)/shard_map/all_gather | solution.py:149
  8.0 571.0 %all-gather.9.cloned.1.call-start = ((), (), s32[]{:S(2)}) async-start(), calls=%async_computation.6 | async-start | bytes 16842752 | tf_op jit(solution)/shard_map/all_gather | solution.py:155
  8.7 2.3 copy-start.15
  8.8 2.3 copy-start.16
  8.8 3.1 copy-start.12
  8.8 3.1 copy-start.3
  12.5 1.8 copy-start.19
  12.5 1.9 copy-start.18
  15.2 1.6 copy-start.5
  33.2 20.9 %copy-start.1 = (bf16[48,32,32,1]{0,3,2,1:T(2,128)(2,1)S(1)}, bf16[48,32,32,1]{0,3,2,1:T(2,128)(2,1)}, u32[]{:S(2)}) copy-start(bf16[48,32,32,1]{0,3,2,1:T(2,128)(2,1)} %get-tuple-element.122) | copy-start | bytes 294916
  38.7 17.4 %copy-start.6 = (f32[48,32]{0,1:T(8,128)S(1)}, f32[48,32]{0,1:T(8,128)}, u32[]{:S(2)}) copy-start(f32[48,32]{0,1:T(8,128)} %copy-done.5) | copy-start | bytes 18436
  38.7 17.4 %copy-start.10 = (f32[64]{0:T(128)S(1)}, f32[64]{0:T(128)}, u32[]{:S(2)}) copy-start(f32[64]{0:T(128)} %get-tuple-element.135) | copy-start | bytes 772
  38.7 17.4 %copy-start.11 = (f32[64]{0:T(128)S(1)}, f32[64]{0:T(128)}, u32[]{:S(2)}) copy-start(f32[64]{0:T(128)} %get-tuple-element.140) | copy-start | bytes 772
  38.7 27.5 %all-to-all-start.1 = ((bf16[128,2,384]{2,1,0:T(2,128)(2,1)}), bf16[128,2,384]{2,1,0:T(2,128)(2,1)}, u32[]{:S(2)}, u32[]{:S(2)}) async-start(bf16[128,2,384]{2,1,0:T(2,128)(2,1)} %reshape.368), calls=%async_computation.1 | async-start | bytes 393216 | tf_op jit(solution)/shard_map/all_to_all | solution.py:101
  56.0 0.8 copy-start.8
  63.9 14.3 %copy-start.4 = (bf16[1,48,2048]{2,1,0:T(8,128)(2,1)S(1)}, bf16[1,48,2048]{2,1,0:T(8,128)(2,1)}, u32[]{:S(2)}) copy-start(bf16[1,48,2048]{2,1,0:T(8,128)(2,1)} %param.24) | copy-start | bytes 589828
  66.2 35.6 %all-to-all-start = ((bf16[128,2,1536]{2,1,0:T(2,128)(2,1)}), bf16[128,2,1536]{2,1,0:T(2,128)(2,1)}, u32[]{:S(2)}, u32[]{:S(2)}) async-start(bf16[128,2,1536]{2,1,0:T(2,128)(2,1)} %reshape.366), calls=%async_computation | async-start | bytes 1572864 | tf_op jit(solution)/shard_map/all_to_all | solution.py:102
  101.8 32.1 %all-to-all-start.2 = ((bf16[128,2,1536]{2,1,0:T(2,128)(2,1)}), bf16[128,2,1536]{2,1,0:T(2,128)(2,1)}, u32[]{:S(2)}, u32[]{:S(2)}) async-start(bf16[128,2,1536]{2,1,0:T(2,128)(2,1)} %reshape.370), calls=%async_computation.2 | async-start | bytes 1572864 | tf_op jit(solution)/shard_map/all_to_all | solution.py:103
  171.5 11.3 %copy-start.13 = (bf16[512]{0:T(512)(128)(2,1)S(1)}, bf16[512]{0:T(512)(128)(2,1)}, u32[]{:S(2)}) copy-start(bf16[512]{0:T(512)(128)(2,1)} %param.29) | copy-start | bytes 3076
  171.5 12.0 %copy-start.14 = (f32[2,50]{1,0:T(2,128)S(1)}, f32[2,50]{1,0:T(2,128)}, u32[]{:S(2)}) copy-start(f32[2,50]{1,0:T(2,128)} %param.36) | copy-start | bytes 1204
  174.5 20.8 %all-to-all-start.3 = ((bf16[128,2,384]{2,1,0:T(2,128)(2,1)}), bf16[128,2,384]{2,1,0:T(2,128)(2,1)S(1)}, u32[]{:S(2)}, u32[]{:S(2)}) async-start(bf16[128,2,384]{2,1,0:T(2,128)(2,1)} %reshape.372), calls=%async_computation.3 | async-start | bytes 393216 | tf_op jit(solution)/shard_map/all_to_all | solution.py:143
  454.2 144.8 %copy-start.2 = (bf16[1,48,3072]{2,1,0:T(8,128)(2,1)S(1)}, bf16[1,48,3072]{2,1,0:T(8,128)(2,1)}, u32[]{:S(2)}) copy-start(bf16[1,48,3072]{2,1,0:T(8,128)(2,1)} %param.21) | copy-start | bytes 884740
  598.9 8.9 %copy-start.17 = (f32[64]{0:T(128)S(1)}, f32[64]{0:T(128)}, u32[]{:S(2)}) copy-start(f32[64]{0:T(128)} %param.34) | copy-start | bytes 772
  607.5 4.9 copy-start.7
  607.5 4.9 copy-start.9
  608.2 4.2 collective-permute-start
Sparse Core Ops, SparseCore 0:
  9.2 221.9 all-gather.4
  233.1 216.5 all-gather.6
  453.4 125.5 all-gather.8
where the time goes:
time: 632 us; the launch traced here: 622 us
  waiting for transfers between devices  412 us (65%)
  local copies, waits for them, and re-layouts  64.4 us (10%)
  starting transfers between devices  47.2 us (7%)
  matrix products  41.1 us (7%)
  other arithmetic  40.8 us (6%)
  between operations  15.6 us (2%)
    all_gather x1, waiting for transfers between devices, on_device(): lax.all_gather(mod_table, 'seq', axis=1, tiled=True)  216 us
    all_gather x1, waiting for transfers between devices, on_device(): lax.all_gather(out_weight, ('cfg', 'seq'), axis=1, tiled=True)  125 us
    unnamed x54, local copies, waits for them, and re-layouts  40.2 us
    all_gather x1, waiting for transfers between devices, on_device(): lax.all_gather(gate_table, 'seq', axis=1, tiled=True)  33.6 us
    dot_general x12, matrix products, key_step(): jnp.einsum('qgd,kgd->gqk', query_all, key_block, preferred_element_type=j...  19.8 us
    all_to_all x1, starting transfers between devices, on_device(): lax.all_to_all(query_send, 'seq', split_axis=0, concat_axis=0, tiled=True)  15.3 us
    all_to_all x1, waiting for transfers between devices, on_device(): lax.all_to_all(key_send, 'seq', split_axis=0, concat_axis=0, tiled=True)  15.1 us
  transfers between devices with their start and end apart: 8, of which 8 were waited for; matrix products, arithmetic and copies ran while one was open for 18% of the time, Pallas kernels for 0%

commit v1 on v0

--- a/solution.py
+++ b/solution.py
@@ -152,7 +152,15 @@
     modulation = jnp.dot(embed_act, mod_full, preferred_element_type=jnp.float32)[0]
     projected = jnp.dot(
         attended_rows,
-        lax.all_gather(out_weight, ("cfg", "seq"), axis=1, tiled=True),
+        jnp.concatenate(
+            lax.all_to_all(
+                jnp.stack([out_weight for _ in range(lax.psum(1, ("cfg", "seq")))], axis=0),
+                ("cfg", "seq"),
+                split_axis=0,
+                concat_axis=0,
+            ),
+            axis=1,
+        ),
         preferred_element_type=jnp.float32,
     )
     model_width = hidden.shape[2]

time: 632 us -> 795 us (1.26)
  waiting for transfers between devices: 412 us -> 547 us
  blocking collectives: 0 us -> 19.4 us
    all_gather x1, waiting for transfers between devices: 33.6 us -> 264 us  [on_device(): lax.all_gather(gate_table, 'seq', axis=1, tiled=True)]
    all_gather x1 -> x0, waiting for transfers between devices: 125 us -> none  [on_device(): lax.all_gather(out_weight, ('cfg', 'seq'), axis=1, tiled=True)]
    all_gather x1, waiting for transfers between devices: 216 us -> 258 us  [on_device(): lax.all_gather(mod_table, 'seq', axis=1, tiled=True)]
    unnamed x54 -> x55, local copies, waits for them, and re-layouts: 40.2 us -> 19.6 us
    reshape x0 -> x1, local copies, waits for them, and re-layouts: none -> 20 us  [on_device(): jnp.concatenate(lax.all_to_all(jnp.stack([out_weight for _ in range(lax.p...]
    all_to_all x0 -> x1, blocking collectives: none -> 19.4 us  [on_device(): lax.all_to_all(back_send, 'seq', split_axis=0, concat_axis=0, tiled=True)]
    all_to_all x1, waiting for transfers between devices: 11.7 us -> 0.01 us  [on_device(): lax.all_to_all(jnp.stack([out_weight for _ in range(lax.psum(1, ('cfg', '...]
  transfers between devices with their start and end apart: 8 -> 7, of which waited for: 8 -> 6; matrix products, arithmetic and copies ran while one was open for 18% -> 6% of each run, Pallas kernels for 0% -> 0%
where the time goes in v1:
time: 795 us; the launch traced here: 783 us
  waiting for transfers between devices  547 us (69%)
  local copies, waits for them, and re-layouts  69.7 us (9%)
  starting transfers between devices  48.5 us (6%)
  matrix products  41.1 us (5%)
  other arithmetic  40.5 us (5%)
  blocking collectives  19.4 us (2%)
  between operations  15.9 us (2%)
    all_gather x1, waiting for transfers between devices, on_device(): lax.all_gather(gate_table, 'seq', axis=1, tiled=True)  264 us
    all_gather x1, waiting for transfers between devices, on_device(): lax.all_gather(mod_table, 'seq', axis=1, tiled=True)  258 us
    reshape x1, local copies, waits for them, and re-layouts, on_device(): jnp.concatenate(lax.all_to_all(jnp.stack([out_weight for _ in range(lax.p...  20 us
    dot_general x12, matrix products, key_step(): jnp.einsum('qgd,kgd->gqk', query_all, key_block, preferred_element_type=j...  19.8 us
    unnamed x55, local copies, waits for them, and re-layouts  19.6 us
    all_to_all x1, blocking collectives, on_device(): lax.all_to_all(back_send, 'seq', split_axis=0, concat_axis=0, tiled=True)  19.4 us
  transfers between devices with their start and end apart: 7, of which 6 were waited for; matrix products, arithmetic and copies ran while one was open for 6% of the time, Pallas kernels for 0%

profile of v1, /device:TPU:1, one launch (start us, length us, event | category | flops | bytes accessed | tf_op | source)
XLA Modules:
  0.0 782.6 jit_solution(6987173073581660519)
XLA Ops:
  6.5 1.2 copy.95
  7.9 1.0 copy.97
  12.9 0.8 multiply_add_fusion
  13.9 0.8 multiply_add_fusion.1
  14.7 3.5 multiply_subtract_fusion
  18.2 1.4 pad_maximum_fusion.1
  19.5 2.1 copy.96
  21.7 2.2 reshape.338
  23.9 1.6 copy.99
  25.5 1.3 rsqrt.30
  26.9 1.3 div.39
  28.2 2.8 fusion.14
  31.0 2.0 copy.101
  33.9 1.7 reduce.27
  35.6 0.7 reshape.376
  36.4 15.3 %all-to-all-start.1 = ((bf16[128,2,384]{2,1,0:T(2,128)(2,1)}), bf16[128,2,384]{2,1,0:T(2,128)(2,1)}, u32[]{:S(2)}, u32[]{:S(2)}) async-start(bf16[128,2,384]{2,1,0:T(2,128)(2,1)} %reshape.376), calls=%async_computation.1 | async-start | bytes 393216 | tf_op jit(solution)/shard_map/all_to_all | solution.py:101
  51.7 1.4 pad_maximum_fusion
  53.7 0.8 fusion.13
  55.3 0.9 all_to_all.36
  56.2 5.3 reduce.26
  61.5 1.5 reshape.374
  63.0 0.9 all-to-all-done.1
  63.8 12.6 %all-to-all-start = ((bf16[128,2,1536]{2,1,0:T(2,128)(2,1)}), bf16[128,2,1536]{2,1,0:T(2,128)(2,1)}, u32[]{:S(2)}, u32[]{:S(2)}) async-start(bf16[128,2,1536]{2,1,0:T(2,128)(2,1)} %reshape.374), calls=%async_computation | async-start | bytes 1572864 | tf_op jit(solution)/shard_map/all_to_all | solution.py:102
  77.2 0.9 all_to_all.38
  78.0 5.3 reduce.28
  83.3 1.4 reshape.378
  84.8 15.0 %all-to-all-done = bf16[128,2,1536]{2,1,0:T(2,128)(2,1)} async-done(((bf16[128,2,1536]{2,1,0:T(2,128)(2,1)}), bf16[128,2,1536]{2,1,0:T(2,128)(2,1)}, u32[]{:S(2)}, u32[]{:S(2)}) %all-to-all-start) | async-done | bytes 786464 | tf_op jit(solution)/shard_map/all_to_all | solution.py:102
  99.8 7.8 all-to-all-start.2
  108.2 1.6 reshape.377
  109.8 1.2 reduce.9
  111.4 5.0 reshape.375
  116.4 4.7 reduce.6
  121.2 1.0 reshape.325
  122.2 1.4 copy.105
  123.6 7.3 all-to-all-done.2
  130.9 5.3 reshape.379
  136.2 4.7 reduce.10
  140.9 1.0 reshape.328
  142.6 25.9 %while.13 = (s32[]{:T(128)}, f32[1,1536,64]{1,2,0:T(8,128)S(1)}, f32[1,1536]{1,0:T(1,128)S(1)}, pred[12,512]{1,0:T(8,128)(4,1)S(1)}, bf16[12,512,1,64]{1,3,2,0:T...) while((s32[]{:T(128)}, f32[1,1536,64]{1,2,0:T(8,128)S(1)}, ...), condition=%wide.region_6.7_spmd.clone, body=%wide.region_4.6_spmd.clone.sunk | while | flops 204670464 | bytes 4286076 | solution.py:139
  142.6 1.6 fusion.47
  144.8 1.6 fusion.47
  147.0 1.6 fusion.47
  149.1 1.6 fusion.47
  151.3 1.6 fusion.47
  153.5 1.6 fusion.47
  155.6 1.6 fusion.47
  157.8 1.6 fusion.47
  159.9 1.6 fusion.47
  162.1 1.6 fusion.47
  164.3 1.6 fusion.47
  166.4 1.6 fusion.47
  169.1 1.7 reduce.29
  170.9 19.4 %all_to_all.45 = bf16[128,2,384]{2,1,0:T(2,128)(2,1)S(1)} all-to-all(bf16[128,2,384]{2,1,0:T(2,128)(2,1)S(1)} %reshape.380), channel_id=1, replica_groups=mesh['cfg'=2,'seq'=128] {'seq'}, dimensions={0} | all-to-all | bytes 393216 | tf_op jit(solution)/shard_map/all_to_all | solution.py:143
  190.3 5.9 stack.8
  196.2 8.3 %all-to-all-start.4 = ((bf16[256,2048,12]{1,2,0:T(8,128)(2,1)}), bf16[256,2048,12]{1,2,0:T(8,128)(2,1)}, u32[]{:S(2)}, u32[]{:S(2)}) async-start(bf16[256,2048,12]{1,2,0:T(8,128)(2,1)} %stack.8), calls=%async_computation.4 | async-start | bytes 33554432 | tf_op jit(solution)/shard_map/all_to_all | solution.py:156
  206.9 1.2 reduce.12
  209.0 264.3 %all-gather.3.cloned.1.call-done = bf16[512,3072]{0,1:T(8,128)(2,1)} async-done(((bf16[512,24]{0,1:T(8,128)(2,1)}), bf16[512,3072]{0,1:T(8,128)(2,1)}) %all-gather.3.cloned.1.call-update) | async-done | bytes 3145744 | tf_op jit(solution)/shard_map/all_gather | solution.py:148
  473.4 2.8 fusion.30
  476.2 257.8 %all-gather.5.cloned.1.call-done = bf16[512,6144]{0,1:T(8,128)(2,1)} async-done(((bf16[512,48]{0,1:T(8,128)(2,1)}), bf16[512,6144]{0,1:T(8,128)(2,1)}) %all-gather.5.cloned.1.call-update) | async-done | bytes 6291472 | tf_op jit(solution)/shard_map/all_gather | solution.py:149
  733.9 4.5 fusion.31
  738.5 20.0 %reshape.332 = bf16[2048,3072]{0,1:T(8,128)(2,1)} reshape(bf16[2048,256,12]{0,2,1:T(8,128)(2,1)} %bitcast.23) | data formatting | bytes 25165824 | tf_op jit(solution)/shard_map/reshape | solution.py:155
  758.4 8.6 %fusion.29 = (f32[48]{0:T(128)S(1)}, f32[48,3072]{1,0:T(8,128)S(1)}) fusion(bf16[48,2048]{1,0:T(8,128)(2,1)S(1)} %reshape.330, bf16[2048,3072]{0,1:T(8,128)(2,1)} %reshape.332, f32[3072]{0:T(1024)S(1)} %bitcast.101, bf16[1,48,3072]{2,1,0:T(8,128)(2,1)S(1)} %copy-done.2), kind=kOutput, calls=%fused_computation.81 | convolution fusion | flops 604569536 | bytes 13676736 | tf_op jit(solution)/shard_map/dot_general | solution.py:153
  767.7 4.3 collective-permute-start
  773.2 1.4 add_select_fusion
  (143 shorter events, 19.7 us)
Async XLA Ops:
  6.5 760.8 %copy-start = (bf16[3072,64]{0,1:T(8,128)(2,1)S(1)}, bf16[3072,64]{0,1:T(8,128)(2,1)}, u32[]{:S(2)}) copy-start(bf16[3072,64]{0,1:T(8,128)(2,1)} %param.33) | copy-start | bytes 1179652
  7.9 2.0 copy-start.16
  7.9 2.0 copy-start.17
  7.9 2.8 copy-start.13
  7.9 2.8 copy-start.3
  11.0 1.8 copy-start.20
  11.4 2.2 copy-start.19
  12.1 2.6 copy-start.5
  31.0 20.7 %copy-start.1 = (bf16[48,32,32,1]{0,3,2,1:T(2,128)(2,1)S(1)}, bf16[48,32,32,1]{0,3,2,1:T(2,128)(2,1)}, u32[]{:S(2)}) copy-start(bf16[48,32,32,1]{0,3,2,1:T(2,128)(2,1)} %get-tuple-element.122) | copy-start | bytes 294916
  36.4 17.4 %copy-start.6 = (f32[48,32]{0,1:T(8,128)S(1)}, f32[48,32]{0,1:T(8,128)}, u32[]{:S(2)}) copy-start(f32[48,32]{0,1:T(8,128)} %copy-done.5) | copy-start | bytes 18436
  36.4 17.4 %copy-start.11 = (f32[64]{0:T(128)S(1)}, f32[64]{0:T(128)}, u32[]{:S(2)}) copy-start(f32[64]{0:T(128)} %get-tuple-element.135) | copy-start | bytes 772
  36.4 17.4 %copy-start.12 = (f32[64]{0:T(128)S(1)}, f32[64]{0:T(128)}, u32[]{:S(2)}) copy-start(f32[64]{0:T(128)} %get-tuple-element.140) | copy-start | bytes 772
  36.4 27.5 %all-to-all-start.1 = ((bf16[128,2,384]{2,1,0:T(2,128)(2,1)}), bf16[128,2,384]{2,1,0:T(2,128)(2,1)}, u32[]{:S(2)}, u32[]{:S(2)}) async-start(bf16[128,2,384]{2,1,0:T(2,128)(2,1)} %reshape.376), calls=%async_computation.1 | async-start | bytes 393216 | tf_op jit(solution)/shard_map/all_to_all | solution.py:101
  53.7 0.8 copy-start.9
  61.5 14.9 %copy-start.4 = (bf16[1,48,2048]{2,1,0:T(8,128)(2,1)S(1)}, bf16[1,48,2048]{2,1,0:T(8,128)(2,1)}, u32[]{:S(2)}) copy-start(bf16[1,48,2048]{2,1,0:T(8,128)(2,1)} %param.24) | copy-start | bytes 589828
  63.8 35.9 %all-to-all-start = ((bf16[128,2,1536]{2,1,0:T(2,128)(2,1)}), bf16[128,2,1536]{2,1,0:T(2,128)(2,1)}, u32[]{:S(2)}, u32[]{:S(2)}) async-start(bf16[128,2,1536]{2,1,0:T(2,128)(2,1)} %reshape.374), calls=%async_computation | async-start | bytes 1572864 | tf_op jit(solution)/shard_map/all_to_all | solution.py:102
  99.8 31.2 %all-to-all-start.2 = ((bf16[128,2,1536]{2,1,0:T(2,128)(2,1)}), bf16[128,2,1536]{2,1,0:T(2,128)(2,1)}, u32[]{:S(2)}, u32[]{:S(2)}) async-start(bf16[128,2,1536]{2,1,0:T(2,128)(2,1)} %reshape.378), calls=%async_computation.2 | async-start | bytes 1572864 | tf_op jit(solution)/shard_map/all_to_all | solution.py:103
  168.6 21.7 %copy-start.7 = (bf16[2048,12]{0,1:T(8,128)(2,1)S(1)}, bf16[2048,12]{0,1:T(8,128)(2,1)}, u32[]{:S(2)}) copy-start(bf16[2048,12]{0,1:T(8,128)(2,1)} %param.32) | copy-start | bytes 147460
  196.2 9.8 %copy-start.14 = (bf16[512]{0:T(512)(128)(2,1)S(1)}, bf16[512]{0:T(512)(128)(2,1)}, u32[]{:S(2)}) copy-start(bf16[512]{0:T(512)(128)(2,1)} %param.29) | copy-start | bytes 3076
  196.2 10.4 %copy-start.15 = (f32[2,50]{1,0:T(2,128)S(1)}, f32[2,50]{1,0:T(2,128)}, u32[]{:S(2)}) copy-start(f32[2,50]{1,0:T(2,128)} %param.36) | copy-start | bytes 1204
  196.2 542.2 %all-to-all-start.4 = ((bf16[256,2048,12]{1,2,0:T(8,128)(2,1)}), bf16[256,2048,12]{1,2,0:T(8,128)(2,1)}, u32[]{:S(2)}, u32[]{:S(2)}) async-start(bf16[256,2048,12]{1,2,0:T(8,128)(2,1)} %stack.8), calls=%async_computation.4 | async-start | bytes 33554432 | tf_op jit(solution)/shard_map/all_to_all | solution.py:156
  204.5 268.9 %all-gather.3.cloned.1.call-start = ((), (), s32[]{:S(2)}) async-start(), calls=%async_computation.5 | async-start | bytes 3170304 | tf_op jit(solution)/shard_map/all_gather | solution.py:148
  205.2 528.7 %all-gather.5.cloned.1.call-start = ((), (), s32[]{:S(2)}) async-start(), calls=%async_computation.6 | async-start | bytes 6340608 | tf_op jit(solution)/shard_map/all_gather | solution.py:149
  738.5 20.0 %copy-start.2 = (bf16[1,48,3072]{2,1,0:T(8,128)(2,1)S(1)}, bf16[1,48,3072]{2,1,0:T(8,128)(2,1)}, u32[]{:S(2)}) copy-start(bf16[1,48,3072]{2,1,0:T(8,128)(2,1)} %param.21) | copy-start | bytes 884740
  758.4 8.9 %copy-start.18 = (f32[64]{0:T(128)S(1)}, f32[64]{0:T(128)}, u32[]{:S(2)}) copy-start(f32[64]{0:T(128)} %param.34) | copy-start | bytes 772
  767.0 6.2 copy-start.8
  767.0 6.2 copy-start.10
  767.7 5.5 collective-permute-start
Sparse Core Ops, SparseCore 0:
  207.2 266.1 all-gather.2
  475.2 258.6 all-gather.4
